TPU v7x, 256 devices: a whole 4x4x8 slice. The times are simulated.
256 devices in a mesh: tm: 32 (over x, z), space: 8 (over y, core).
Axes of the slice: x: 4, y: 4, z: 8, core: 2. Of those that a mesh axis runs over, the one named last changes fastest.
Arguments:
- increment: float32 [128, 4, 64, 512], P('tm', None, 'space'), may hold values from -6 to 6
- trajectory: float32 [128, 4, 64, 512], P('tm', None, 'space'), may hold values from -6 to 6
- input_weight: float32 [32, 4, 3, 3], replicated, may hold values from -1 to 1
- bias: float32 [32], replicated, may hold values from -4 to 4
- output_weight: float32 [4, 32, 3, 3], replicated, may hold values from -0.375 to 0.375
- correlation: float32 [4, 128, 128], replicated, may hold values from -1 to 4, as said below
Outputs:
- corrected: float32 [128, 4, 64, 512], P('tm', None, 'space')
Inputs may be any that keep to these rules, and one draw needn't show every extreme that they name: `correlation`: each field's matrix is symmetric positive definite.
All inputs are finite; a program needn't handle non-finite values.
Results may differ from a plain program's by a relative error of at most 0.0001.
Values sent between devices are 32-bit elements; how exact they have to be, the bound alone decides.
A program may use at most 64 MiB of HBM per device.

v0:
```python
import functools

import jax
import jax.numpy as jnp
import numpy as np
from jax import lax
from jax.experimental import pallas as pl
from jax.experimental.pallas import tpu as pltpu
from jax.sharding import PartitionSpec as P

MESH = pl.DeviceIdType.MESH
F32, BF16 = jnp.float32, jnp.bfloat16
VMEM = pl.BlockSpec(memory_space=pltpu.VMEM)
HBM = pl.BlockSpec(memory_space=pl.ANY)

ROWS, FIELDS, CHANNELS = 8, 4, 32
PAIR = 2 * FIELDS
TAPS = 48
HALVES = ((-3, 3), (-1, 3))


def tap(a, b, f):
    return (a * 3 + b) * FIELDS + f


def selections():
    wide = np.zeros((4, 2 * TAPS, 9 * 3 * PAIR), np.float32)
    narrow = np.zeros((2, 2 * TAPS, 6 * 3 * PAIR), np.float32)
    for table, pairs in ((wide, 3), (narrow, 2)):
        third = pairs * 3 * PAIR
        for i in range(table.shape[0]):
            for k in range(pairs):
                for b in range(3):
                    for f in range(FIELDS):
                        for r in range(2):
                            a = 2 * k + r - i
                            if 0 <= a < 3:
                                line = (k * 3 + b) * PAIR + 2 * f + r
                                table[i, tap(a, b, f), line] = 1.0
                                table[i, tap(a, b, f), third + line] = 1.0
                                table[i, TAPS + tap(a, b, f), 2 * third + line] = 1.0
    out = np.zeros((2, 9 * PAIR, 4 * TAPS), np.float32)
    for k in range(3):
        for b in range(3):
            for f in range(FIELDS):
                for r in range(2):
                    for a in range(3):
                        i = 2 * k + r + a
                        out[i // 4, (k * 3 + b) * PAIR + 2 * f + r, i % 4 * TAPS + tap(a, b, f)] = 1.0
    return wide, narrow, out


def split(x):
    high = x.astype(BF16)
    return high, (x - high.astype(F32)).astype(BF16)


def dot(a, b):
    return jnp.dot(a, b, preferred_element_type=F32)


def three(ah, al, bh, bl):
    return dot(ah, bh) + dot(al, bh) + dot(ah, bl)


def cycle_kernel(
    inc_hbm, traj_hbm, w_in, w_bias, w_out, pick_wide, pick_narrow, pick_out, perm, corr,
    out,
    inc, traj, up, down, top, bot,
    taps_in, taps_out, bias, t1, t1n, t2h, t2l,
    xs, hh, hl, fore, before, rows, cols, results, back, cmat,
    in_sem, c_sem, halo_send, halo_recv, nb_send, nb_recv, f_send, f_recv, b_send, b_recv,
):
    slots, nx = inc.shape[0], inc.shape[3]
    quarter = nx // 128
    depth = lax.axis_size("tm")
    width = depth // FIELDS
    me = lax.axis_index("tm")
    my_field, my_row = lax.div(me, width), lax.rem(me, width)
    place = lax.axis_index("space")
    last = lax.axis_size("space") - 1
    order = [slots - 1] + list(range(slots - 1))

    barrier = pltpu.get_barrier_semaphore()

    def peer_of(p):
        return lax.rem(my_field + lax.div(p, width), FIELDS) * width + lax.rem(my_row + lax.rem(p, width), width)

    @pl.when(place > 0)
    def _():
        pl.semaphore_signal(barrier, inc=1, device_id={"space": place - 1}, device_id_type=MESH)

    @pl.when(place < last)
    def _():
        pl.semaphore_signal(barrier, inc=1, device_id={"space": place + 1}, device_id_type=MESH)

    def inputs(j):
        return (
            pltpu.make_async_copy(traj_hbm.at[j], traj.at[j], in_sem.at[0, j]),
            pltpu.make_async_copy(inc_hbm.at[j], inc.at[j], in_sem.at[1, j]),
        )

    for j in order:
        for copy in inputs(j):
            copy.start()

    @pl.loop(1, depth)
    def _(p):
        pl.semaphore_signal(barrier, inc=1, device_id={"tm": peer_of(p)}, device_id_type=MESH)

    c_copy = pltpu.make_async_copy(corr.at[my_field], cmat, c_sem)
    c_copy.start()

    def pack(j):
        for array, source in enumerate((traj, inc)):
            for f in range(FIELDS):
                for half, target in enumerate((up, down)):
                    for k in range(2):
                        r = 4 * half + 2 * k
                        target[j, array, PAIR * k + 2 * f : PAIR * k + 2 * f + 2, :] = source[j, f, r : r + 2, :]

    def to_next(j):
        return pltpu.make_async_remote_copy(
            down.at[j], top.at[j], halo_send.at[0, j], halo_recv.at[0, j],
            device_id={"space": place + 1}, device_id_type=MESH,
        )

    def to_previous(j):
        return pltpu.make_async_remote_copy(
            up.at[j], bot.at[j], halo_send.at[1, j], halo_recv.at[1, j],
            device_id={"space": place - 1}, device_id_type=MESH,
        )

    for n, j in enumerate(order):
        for copy in inputs(j):
            copy.wait()
        pack(j)
        if n == 0:
            pl.semaphore_wait(barrier, depth - 1 + jnp.minimum(place, 1) + jnp.minimum(last - place, 1))

        @pl.when(place < last)
        def _():
            to_next(j).start()

        @pl.when(place > 0)
        def _():
            to_previous(j).start()

    taps_in[...] = jnp.zeros_like(taps_in)
    taps_out[...] = jnp.zeros_like(taps_out)
    for a in range(3):
        for b in range(3):
            at = tap(a, b, 0)
            taps_in[at : at + FIELDS, :CHANNELS] = w_in[a, b]
            w = 0.5 * w_out[a, b]
            for q in range(4):
                taps_out[q * TAPS + at : q * TAPS + at + FIELDS, q * CHANNELS : q * CHANNELS + CHANNELS] = w
    taps_in[2 * TAPS : 2 * TAPS + 1, :CHANNELS] = w_bias[...]
    w = taps_in[:TAPS, :]
    high = w.astype(BF16).astype(F32)
    taps_in[:TAPS, :] = high
    taps_in[TAPS : 2 * TAPS, :] = w - high
    w = jnp.transpose(taps_in[...])[:CHANNELS]
    bias[...] = jnp.broadcast_to(w[:, 2 * TAPS : 2 * TAPS + 1], (CHANNELS, 128))
    w = w[:, : 2 * TAPS].astype(BF16)
    for i in range(4):
        t1[CHANNELS * i : CHANNELS * i + CHANNELS, :] = dot(w, pick_wide[i]).astype(BF16)
    for i in range(2):
        t1n[CHANNELS * i : CHANNELS * i + CHANNELS, :] = dot(w, pick_narrow[i]).astype(BF16)
    lane_row = lax.shift_right_logical(lax.broadcasted_iota(jnp.int32, (1, 128), 1), 5) + place * ROWS
    for part, target in zip(split(taps_out[...]), (t2h, t2l)):
        for g in range(2):
            x = dot(pick_out[g], part)
            for step_id in range(2):
                for half in range(2):
                    row = lane_row + (HALVES[step_id][half] + 4 * g)
                    keep = jnp.where((row >= 0) & (row < (last + 1) * ROWS), x, 0.0)
                    target[step_id, half, :, 128 * g : 128 * g + 128] = keep.astype(BF16)

    @pl.when(place == 0)
    def _():
        top[...] = jnp.zeros_like(top)

    @pl.when(place == last)
    def _():
        bot[...] = jnp.zeros_like(bot)

    column = lax.broadcasted_iota(jnp.int32, (1, nx), 1)
    first, final = column == 0, column == nx - 1

    def step(state, step_id):
        pairs = len(state[0])
        outs = pairs - 2
        mids = 2 * outs + 2
        highs, lows = [], []
        for k in range(pairs):
            high, low = [], []
            for array in range(2):
                x = state[array][k]
                left = jnp.where(first, 0.0, pltpu.roll(x, 1, 1))
                right = jnp.where(final, 0.0, pltpu.roll(x, nx - 1, 1))
                x = jnp.concatenate([left, x, right], axis=0)
                h = x.astype(BF16).astype(F32)
                high.append(h)
                low.append(x - h)
            highs.append(jnp.concatenate(high, axis=1))
            lows.append(jnp.concatenate(low, axis=1))
        at = 0
        spans = [(g, 3) for g in range(0, pairs - 2, 2)] + [(pairs - 2, 2)]
        for g, n in spans:
            high = highs[g : g + n]
            value = jnp.concatenate(high + lows[g : g + n] + high, axis=0).astype(BF16)
            xs[g // 2, : value.shape[0], :] = value
        b = jnp.concatenate([bias[...], bias[...]], axis=1)[None]
        for n in range(0, nx, 256):
            s, t = slice(n, n + 256), slice(nx + n, nx + n + 256)
            at = 0
            for g, count in spans:
                table, many = (t1, 4) if count == 3 else (t1n, 2)
                depth_in = 9 * count * PAIR
                zs = dot(table[...], xs[g // 2, :depth_in, s])
                zt = dot(table[...], xs[g // 2, :depth_in, t])
                h = jnp.tanh(zs.reshape(many, CHANNELS, 256) + b).reshape(many * CHANNELS, 256)
                slope = (1.0 - h * h) * zt
                lines = slice(at, at + many * CHANNELS)
                hh[lines, s], hl[lines, s] = split(h)
                hh[lines, t], hl[lines, t] = split(slope)
                at += many * CHANNELS
        new = [[], []]
        wide, deep = outs // 2, (outs + 2) * CHANNELS
        for array in range(2):
            lane = slice(array * nx, array * nx + nx)
            for half in range(2):
                start = half * outs * CHANNELS
                taps = three(
                    t2h[step_id, half, : 3 * PAIR * wide, :deep],
                    t2l[step_id, half, : 3 * PAIR * wide, :deep],
                    hh[start : start + deep, lane],
                    hl[start : start + deep, lane],
                )
                for k in range(wide):
                    left = jnp.where(first, 0.0, pltpu.roll(taps[3 * PAIR * k : 3 * PAIR * k + PAIR], 1, 1))
                    middle = taps[3 * PAIR * k + PAIR : 3 * PAIR * k + 2 * PAIR]
                    right = pltpu.roll(taps[3 * PAIR * k + 2 * PAIR : 3 * PAIR * k + 3 * PAIR], nx - 1, 1)
                    right = jnp.where(final, 0.0, right)
                    new[array].append(state[array][half * wide + k + 1] + (left + middle + right))
        return new

    def line_of(device):
        f, r = lax.div(device, width), lax.rem(device, width)
        return lax.div(r, 2) * PAIR + 2 * f + lax.rem(r, 2)

    def send_residual(j, value):
        for q in range(quarter):
            rows[j, :, q, :] = value[:, 128 * q : 128 * q + 128]
        pltpu.make_async_copy(rows.at[j, line_of(me)], cols.at[j, me], f_recv.at[j]).start()

        @pl.loop(1, depth)
        def _(p):
            peer = peer_of(p)
            pltpu.make_async_remote_copy(
                rows.at[j, line_of(peer)], cols.at[j, me], f_send.at[j], f_recv.at[j],
                device_id={"tm": peer}, device_id_type=MESH,
            ).start()

    def increment_lines(j):
        return jnp.concatenate([up[j, 1], down[j, 1]], axis=0)

    after = lax.rem(me + 1, depth)
    to_after = pltpu.make_async_remote_copy(fore, before, nb_send, nb_recv, device_id={"tm": after}, device_id_type=MESH)

    @pl.loop(0, slots)
    def _(i):
        slot = lax.rem(i + slots - 1, slots)

        @pl.when(place > 0)
        def _():
            to_next(slot).wait_recv()

        @pl.when(place < last)
        def _():
            to_previous(slot).wait_recv()

        state = []
        for array in range(2):
            parts = [x[slot, array] for x in (top, up, down, bot)]
            state.append([x[PAIR * k : PAIR * k + PAIR] for x in parts for k in range(2)])
        state = step(state, 0)
        for array in range(2):
            state[array][0] = jnp.where(place > 0, state[array][0], 0.0)
            state[array][-1] = jnp.where(place < last, state[array][-1], 0.0)
        state = step(state, 1)
        forecast = jnp.concatenate(state[1], axis=0)

        @pl.when(i == 0)
        def _():
            fore[...] = forecast
            to_after.start()

        @pl.when(i > 0)
        def _():
            send_residual(slot + 1, increment_lines(slot + 1) - forecast)

        @pl.when(i == slots - 2)
        def _():
            to_after.wait()
            earlier = jnp.where(me == 0, 0.0, before[...])
            send_residual(0, increment_lines(0) - earlier)

    c_copy.wait()
    ch, cl = split(cmat[...])
    ch = dot(ch, perm[...]).astype(BF16)
    cl = dot(cl, perm[...]).astype(BF16)
    for j in range(slots):
        pltpu.make_async_copy(cols.at[j], cols.at[j], f_recv.at[j]).wait()
    for q in range(quarter):
        v = jnp.concatenate([cols[j, :, q, :] for j in range(slots)], axis=0)
        results[:, q, :] = three(ch, cl, *split(v))
    mine = pl.ds(me * slots, slots)
    pltpu.make_async_copy(results.at[mine], back.at[mine], b_recv).start()

    @pl.loop(1, depth)
    def _(p):
        peer = peer_of(p)
        pltpu.make_async_remote_copy(
            results.at[pl.ds(peer * slots, slots)], back.at[mine], b_send, b_recv,
            device_id={"tm": peer}, device_id_type=MESH,
        ).start()

    pltpu.make_async_copy(back, back, b_recv).wait()
    lines = back.reshape(depth * slots * quarter, 128)
    for j in range(slots):
        for f in range(FIELDS):
            for q in range(quarter):
                out[j, f, :, 128 * q : 128 * q + 128] = lines[
                    pl.ds((f * width * slots + j) * quarter + q, ROWS, stride=slots * quarter), :
                ]
    rest = pl.ds(0, (depth - 1) * slots)
    pltpu.make_async_copy(results.at[rest], results.at[rest], b_send).wait()
    for j in range(slots):
        pltpu.make_async_copy(rows.at[j, pl.ds(0, depth - 1)], rows.at[j, pl.ds(0, depth - 1)], f_send.at[j]).wait()

        @pl.when(place < last)
        def _():
            to_next(j).wait_send()

        @pl.when(place > 0)
        def _():
            to_previous(j).wait_send()


def body(increment, trajectory, input_weight, bias, output_weight, correlation):
    slots, fields, rows, nx = increment.shape
    pick_wide, pick_narrow, pick_out = (jnp.asarray(x, BF16) for x in selections())
    depth = lax.axis_size("tm")
    time = correlation.shape[1]
    perm = np.zeros((time, time), np.float32)
    for e in range(depth):
        for j in range(slots):
            perm[e * slots + j, j * depth + e] = 1.0
    local = increment.shape
    halo = (slots, 2, 2 * PAIR, nx)
    hidden = (14 * CHANNELS, 2 * nx)
    message = (slots, depth, nx // 128, 128)
    dma = pltpu.SemaphoreType.DMA
    return pl.pallas_call(
        cycle_kernel,
        out_shape=jax.ShapeDtypeStruct(local, F32),
        in_specs=[HBM, HBM] + [VMEM] * 7 + [HBM],
        out_specs=VMEM,
        scratch_shapes=[
            pltpu.VMEM(local, F32),
            pltpu.VMEM(local, F32),
            pltpu.VMEM(halo, F32),
            pltpu.VMEM(halo, F32),
            pltpu.VMEM(halo, F32),
            pltpu.VMEM(halo, F32),
            pltpu.VMEM((128, 128), F32),
            pltpu.VMEM((4 * TAPS, 128), F32),
            pltpu.VMEM((CHANNELS, 128), F32),
            pltpu.VMEM((4 * CHANNELS, 27 * PAIR), BF16),
            pltpu.VMEM((2 * CHANNELS, 18 * PAIR), BF16),
            pltpu.VMEM((2, 2, 9 * PAIR, 256), BF16),
            pltpu.VMEM((2, 2, 9 * PAIR, 256), BF16),
            pltpu.VMEM((4, 27 * PAIR, 2 * nx), BF16),
            pltpu.VMEM(hidden, BF16),
            pltpu.VMEM(hidden, BF16),
            pltpu.VMEM((fields * rows, nx), F32),
            pltpu.VMEM((fields * rows, nx), F32),
            pltpu.VMEM(message, F32),
            pltpu.VMEM(message, F32),
            pltpu.VMEM((time, nx // 128, 128), F32),
            pltpu.VMEM((time, nx // 128, 128), F32),
            pltpu.VMEM((time, time), F32),
            dma((2, slots)), dma, dma((2, slots)), dma((2, slots)),
            dma, dma, dma((slots,)), dma((slots,)), dma, dma,
        ],
        compiler_params=pltpu.CompilerParams(collective_id=0, has_side_effects=True),
        name="cycle",
    )(
        increment, trajectory,
        jnp.transpose(input_weight, (2, 3, 1, 0)), bias[None, :], jnp.transpose(output_weight, (2, 3, 0, 1)),
        pick_wide, pick_narrow, pick_out, jnp.asarray(perm, BF16), correlation,
    )


def solution(mesh):
    split_spec = P("tm", None, "space", None)
    return jax.shard_map(
        body,
        mesh=mesh,
        in_specs=(split_spec, split_spec, P(), P(), P(), P()),
        out_specs=split_spec,
        check_vma=False,
    )
```

profile of v0, /device:TPU:1, one launch (start us, length us, event | category | flops | bytes accessed | tf_op | source)
XLA Modules:
  0.0 42.3 jit_solution(13939660259163887533)
XLA Ops:
  0.0 40.6 %cycle.1 = f32[4,4,8,512]{3,2,1,0:T(8,128)} custom-call(f32[4,4,8,512]{3,2,1,0:T(8,128)} %inc_hbm.1, f32[4,4,8,512]{3,2,1,0:T(8,128)} %traj_hbm.1, f32[3,3,4,32]{3,2,1,0:T(4,128)} %bitcast.3, f32[1,32]{1,0:T(1,128)} %bitcast.5, f32[3,3,4,32]{3,2,1,0:T(4,128)} %bitcast.4, bf16[4,96,216]{2,1,0:T(8,128)(2,1)} %constant.8.clone.pick_wide, ...), custom_call_target="tpu_custom_call" | custom-call | tf_op jit(solution)/shard_map/cycle/pallas_call | solution.py:366
  40.6 1.7 %copy.12 = f32[4,4,8,512]{3,2,1,0:T(8,128)} copy(f32[4,4,8,512]{3,2,1,0:T(8,128)} %cycle.1) | data formatting | bytes 524288
where the time goes:
time: 42.5 us; the launch traced here: 42.3 us
  Pallas kernels  40.6 us (96%)
  local copies, waits for them, and re-layouts  1.67 us (4%)
    pallas_call x1, Pallas kernels, body(): pl.pallas_call(cycle_kernel, out_shape=jax.ShapeDtypeStruct(local, F32),...  40.6 us
    unnamed x1, local copies, waits for them, and re-layouts  1.67 us

commit v1 on v0

--- a/solution.py
+++ b/solution.py
@@ -50,6 +50,12 @@
     return wide, narrow, out
 
 
+def far_first(wide, deep):
+    offsets = [(p, q) for p in range(wide) for q in range(deep) if p or q]
+    hops = lambda n, size: min(n, size - n)
+    return sorted(offsets, key=lambda o: (-hops(o[0], wide) - hops(o[1], deep), -hops(o[1], deep), o))
+
+
 def split(x):
     high = x.astype(BF16)
     return high, (x - high.astype(F32)).astype(BF16)
@@ -83,8 +89,12 @@
 
     barrier = pltpu.get_barrier_semaphore()
 
-    def peer_of(p):
-        return lax.rem(my_field + lax.div(p, width), FIELDS) * width + lax.rem(my_row + lax.rem(p, width), width)
+    fields = [my_field] + [lax.rem(my_field + p, FIELDS) for p in range(1, FIELDS)]
+    strips = [my_row] + [lax.rem(my_row + p, width) for p in range(1, width)]
+    peers = [(fields[p], strips[q]) for p, q in far_first(FIELDS, width)]
+
+    def device(peer):
+        return {"tm": peer[0] * width + peer[1]}
 
     @pl.when(place > 0)
     def _():
@@ -104,9 +114,8 @@
         for copy in inputs(j):
             copy.start()
 
-    @pl.loop(1, depth)
-    def _(p):
-        pl.semaphore_signal(barrier, inc=1, device_id={"tm": peer_of(p)}, device_id_type=MESH)
+    for peer in peers:
+        pl.semaphore_signal(barrier, inc=1, device_id=device(peer), device_id_type=MESH)
 
     c_copy = pltpu.make_async_copy(corr.at[my_field], cmat, c_sem)
     c_copy.start()
@@ -246,22 +255,19 @@
                     new[array].append(state[array][half * wide + k + 1] + (left + middle + right))
         return new
 
-    def line_of(device):
-        f, r = lax.div(device, width), lax.rem(device, width)
+    def line_of(peer):
+        f, r = peer
         return lax.div(r, 2) * PAIR + 2 * f + lax.rem(r, 2)
 
     def send_residual(j, value):
         for q in range(quarter):
             rows[j, :, q, :] = value[:, 128 * q : 128 * q + 128]
-        pltpu.make_async_copy(rows.at[j, line_of(me)], cols.at[j, me], f_recv.at[j]).start()
-
-        @pl.loop(1, depth)
-        def _(p):
-            peer = peer_of(p)
+        for peer in peers:
             pltpu.make_async_remote_copy(
                 rows.at[j, line_of(peer)], cols.at[j, me], f_send.at[j], f_recv.at[j],
-                device_id={"tm": peer}, device_id_type=MESH,
+                device_id=device(peer), device_id_type=MESH,
             ).start()
+        pltpu.make_async_copy(rows.at[j, line_of((my_field, my_row))], cols.at[j, me], f_recv.at[j]).start()
 
     def increment_lines(j):
         return jnp.concatenate([up[j, 1], down[j, 1]], axis=0)
@@ -317,15 +323,12 @@
         v = jnp.concatenate([cols[j, :, q, :] for j in range(slots)], axis=0)
         results[:, q, :] = three(ch, cl, *split(v))
     mine = pl.ds(me * slots, slots)
+    for peer in peers:
+        pltpu.make_async_remote_copy(
+            results.at[pl.ds((peer[0] * width + peer[1]) * slots, slots)], back.at[mine], b_send, b_recv,
+            device_id=device(peer), device_id_type=MESH,
+        ).start()
     pltpu.make_async_copy(results.at[mine], back.at[mine], b_recv).start()
-
-    @pl.loop(1, depth)
-    def _(p):
-        peer = peer_of(p)
-        pltpu.make_async_remote_copy(
-            results.at[pl.ds(peer * slots, slots)], back.at[mine], b_send, b_recv,
-            device_id={"tm": peer}, device_id_type=MESH,
-        ).start()
 
     pltpu.make_async_copy(back, back, b_recv).wait()
     lines = back.reshape(depth * slots * quarter, 128)
@@ -365,7 +368,7 @@
     dma = pltpu.SemaphoreType.DMA
     return pl.pallas_call(
         cycle_kernel,
-        out_shape=jax.ShapeDtypeStruct(local, F32),
+        out_shape=pltpu.VMEM(local, F32),
         in_specs=[HBM, HBM] + [VMEM] * 7 + [HBM],
         out_specs=VMEM,
         scratch_shapes=[

time: 42.5 us -> 37.5 us (0.88); the launches traced: 42.3 us -> 36.9 us
  Pallas kernels: 40.6 us -> 36.2 us
  local copies, waits for them, and re-layouts: 1.67 us -> 0.71 us
    pallas_call x1, Pallas kernels: 40.6 us -> 36.2 us  [body(): pl.pallas_call(cycle_kernel, out_shape=pltpu.VMEM(local, F32), in_specs=[...]
    unnamed x1, local copies, waits for them, and re-layouts: 1.67 us -> 0.71 us
where the time goes in v1:
time: 37.5 us; the launch traced here: 36.9 us
  Pallas kernels  36.2 us (97%)
  local copies, waits for them, and re-layouts  0.71 us (2%)
    pallas_call x1, Pallas kernels, body(): pl.pallas_call(cycle_kernel, out_shape=pltpu.VMEM(local, F32), in_specs=[...  36.2 us

profile of v1, /device:TPU:1, one launch (start us, length us, event | category | flops | bytes accessed | tf_op | source)
XLA Modules:
  0.0 36.9 jit_solution(381579871342362183)
XLA Ops:
  0.0 36.2 %cycle.1 = f32[4,4,8,512]{3,2,1,0:T(8,128)S(1)} custom-call(f32[4,4,8,512]{3,2,1,0:T(8,128)} %inc_hbm.1, f32[4,4,8,512]{3,2,1,0:T(8,128)} %traj_hbm.1, f32[3,3,4,32]{3,2,1,0:T(4,128)} %bitcast.3, f32[1,32]{1,0:T(1,128)} %bitcast.5, f32[3,3,4,32]{3,2,1,0:T(4,128)} %bitcast.4, bf16[4,96,216]{2,1,0:T(8,128)(2,1)} %constant.8.clone.pick_wide, ...), custom_call_target="tpu_custom_call" | custom-call | tf_op jit(solution)/shard_map/cycle/pallas_call | solution.py:369
  36.2 0.7 %copy.12 = f32[4,4,8,512]{3,2,1,0:T(8,128)} copy(f32[4,4,8,512]{3,2,1,0:T(8,128)S(1)} %cycle.1) | data formatting | bytes 524288

commit v2 on v1

--- a/solution.py
+++ b/solution.py
@@ -70,12 +70,20 @@
 
 
 def cycle_kernel(
-    inc_hbm, traj_hbm, w_in, w_bias, w_out, pick_wide, pick_narrow, pick_out, perm, corr,
-    out,
+    inc_hbm, traj_hbm, *refs,
+):
+    count = 7
+    tables_hbm, corr, refs = refs[:count], refs[count], refs[count + 1 :]
+    out, tables, refs = refs[0], refs[1 : count + 1], refs[count + 1 :]
+    cycle(inc_hbm, traj_hbm, tables_hbm, corr, out, tables, *refs)
+
+
+def cycle(
+    inc_hbm, traj_hbm, tables_hbm, corr, out, tables,
     inc, traj, up, down, top, bot,
     taps_in, taps_out, bias, t1, t1n, t2h, t2l,
     xs, hh, hl, fore, before, rows, cols, results, back, cmat,
-    in_sem, c_sem, halo_send, halo_recv, nb_send, nb_recv, f_send, f_recv, b_send, b_recv,
+    in_sem, table_sem, c_sem, met, halo_send, halo_recv, nb_send, nb_recv, f_send, f_recv, b_send, b_recv,
 ):
     slots, nx = inc.shape[0], inc.shape[3]
     quarter = nx // 128
@@ -96,6 +104,15 @@
     def device(peer):
         return {"tm": peer[0] * width + peer[1]}
 
+    beside = [(my_field, strips[1]), (my_field, strips[-1])]
+    across = [(fields[1], my_row), (fields[-1], my_row)]
+
+    def say(sem, devices):
+        for d in devices:
+            pl.semaphore_signal(sem, inc=1, device_id=device(d), device_id_type=MESH)
+
+    w_in, w_bias, w_out, pick_wide, pick_narrow, pick_out, perm = tables
+
     @pl.when(place > 0)
     def _():
         pl.semaphore_signal(barrier, inc=1, device_id={"space": place - 1}, device_id_type=MESH)
@@ -110,13 +127,14 @@
             pltpu.make_async_copy(inc_hbm.at[j], inc.at[j], in_sem.at[1, j]),
         )
 
+    say(barrier, beside + across)
     for j in order:
         for copy in inputs(j):
             copy.start()
 
-    for peer in peers:
-        pl.semaphore_signal(barrier, inc=1, device_id=device(peer), device_id_type=MESH)
-
+    table_copies = [pltpu.make_async_copy(*x, table_sem.at[n]) for n, x in enumerate(zip(tables_hbm, tables))]
+    for copy in table_copies:
+        copy.start()
     c_copy = pltpu.make_async_copy(corr.at[my_field], cmat, c_sem)
     c_copy.start()
 
@@ -145,7 +163,7 @@
             copy.wait()
         pack(j)
         if n == 0:
-            pl.semaphore_wait(barrier, depth - 1 + jnp.minimum(place, 1) + jnp.minimum(last - place, 1))
+            pl.semaphore_wait(barrier, 4 + jnp.minimum(place, 1) + jnp.minimum(last - place, 1))
 
         @pl.when(place < last)
         def _():
@@ -154,6 +172,11 @@
         @pl.when(place > 0)
         def _():
             to_previous(j).start()
+
+    rounds = width // 2 - 1
+    say(met.at[0], beside)
+    for copy in table_copies:
+        copy.wait()
 
     taps_in[...] = jnp.zeros_like(taps_in)
     taps_out[...] = jnp.zeros_like(taps_out)
@@ -169,6 +192,8 @@
     high = w.astype(BF16).astype(F32)
     taps_in[:TAPS, :] = high
     taps_in[TAPS : 2 * TAPS, :] = w - high
+    pl.semaphore_wait(met.at[0], 2)
+    say(met.at[1], beside)
     w = jnp.transpose(taps_in[...])[:CHANNELS]
     bias[...] = jnp.broadcast_to(w[:, 2 * TAPS : 2 * TAPS + 1], (CHANNELS, 128))
     w = w[:, : 2 * TAPS].astype(BF16)
@@ -176,6 +201,9 @@
         t1[CHANNELS * i : CHANNELS * i + CHANNELS, :] = dot(w, pick_wide[i]).astype(BF16)
     for i in range(2):
         t1n[CHANNELS * i : CHANNELS * i + CHANNELS, :] = dot(w, pick_narrow[i]).astype(BF16)
+    for n in range(1, rounds):
+        pl.semaphore_wait(met.at[n], 2)
+        say(met.at[n + 1], beside if n + 1 < rounds else across)
     lane_row = lax.shift_right_logical(lax.broadcasted_iota(jnp.int32, (1, 128), 1), 5) + place * ROWS
     for part, target in zip(split(taps_out[...]), (t2h, t2l)):
         for g in range(2):
@@ -301,7 +329,13 @@
         @pl.when(i == 0)
         def _():
             fore[...] = forecast
+            pl.semaphore_wait(met.at[rounds], 2)
+            say(met.at[rounds + 1], across)
             to_after.start()
+
+        @pl.when(i == 1)
+        def _():
+            pl.semaphore_wait(met.at[rounds + 1], 2)
 
         @pl.when(i > 0)
         def _():
@@ -361,6 +395,10 @@
     for e in range(depth):
         for j in range(slots):
             perm[e * slots + j, j * depth + e] = 1.0
+    tables = (
+        jnp.transpose(input_weight, (2, 3, 1, 0)), bias[None, :], jnp.transpose(output_weight, (2, 3, 0, 1)),
+        pick_wide, pick_narrow, pick_out, jnp.asarray(perm, BF16),
+    )
     local = increment.shape
     halo = (slots, 2, 2 * PAIR, nx)
     hidden = (14 * CHANNELS, 2 * nx)
@@ -369,9 +407,10 @@
     return pl.pallas_call(
         cycle_kernel,
         out_shape=pltpu.VMEM(local, F32),
-        in_specs=[HBM, HBM] + [VMEM] * 7 + [HBM],
+        in_specs=[HBM] * 10,
         out_specs=VMEM,
-        scratch_shapes=[
+        scratch_shapes=[pltpu.VMEM(x.shape, x.dtype) for x in tables]
+        + [
             pltpu.VMEM(local, F32),
             pltpu.VMEM(local, F32),
             pltpu.VMEM(halo, F32),
@@ -395,16 +434,12 @@
             pltpu.VMEM((time, nx // 128, 128), F32),
             pltpu.VMEM((time, nx // 128, 128), F32),
             pltpu.VMEM((time, time), F32),
-            dma((2, slots)), dma, dma((2, slots)), dma((2, slots)),
+            dma((2, slots)), dma((len(tables),)), dma, pltpu.SemaphoreType.REGULAR((8,)), dma((2, slots)), dma((2, slots)),
             dma, dma, dma((slots,)), dma((slots,)), dma, dma,
         ],
         compiler_params=pltpu.CompilerParams(collective_id=0, has_side_effects=True),
         name="cycle",
-    )(
-        increment, trajectory,
-        jnp.transpose(input_weight, (2, 3, 1, 0)), bias[None, :], jnp.transpose(output_weight, (2, 3, 0, 1)),
-        pick_wide, pick_narrow, pick_out, jnp.asarray(perm, BF16), correlation,
-    )
+    )(increment, trajectory, *tables, correlation)
 
 
 def solution(mesh):

time: 37.5 us -> 35.2 us (0.939)
  the two profiles are of different devices: /device:TPU:1 before, /device:TPU:8 now
where the time goes in v2:
time: 35.2 us; the launch traced here: 35.1 us
  Pallas kernels  34.4 us (98%)
  local copies, waits for them, and re-layouts  0.71 us (2%)
    pallas_call x1, Pallas kernels, body(): pl.pallas_call(cycle_kernel, out_shape=pltpu.VMEM(local, F32), in_specs=[...  34.4 us
    unnamed x1, local copies, waits for them, and re-layouts  0.71 us

profile of v2, /device:TPU:8, one launch (start us, length us, event | category | flops | bytes accessed | tf_op | source)
XLA Modules:
  0.0 35.1 jit_solution(1939845149436592479)
XLA Ops:
  0.0 34.4 %cycle.1 = f32[4,4,8,512]{3,2,1,0:T(8,128)S(1)} custom-call(f32[4,4,8,512]{3,2,1,0:T(8,128)} %inc_hbm.1, f32[4,4,8,512]{3,2,1,0:T(8,128)} %traj_hbm.1, f32[3,3,4,32]{3,2,1,0:T(4,128)} %bitcast.3, f32[1,32]{1,0:T(1,128)} %bitcast.5, f32[3,3,4,32]{3,2,1,0:T(4,128)} %bitcast.4, bf16[4,96,216]{2,1,0:T(8,128)(2,1)} %constant.8.clone.refs_3_, ...), custom_call_target="tpu_custom_call" | custom-call | tf_op jit(solution)/shard_map/cycle/pallas_call | solution.py:407
  34.4 0.7 %copy.12 = f32[4,4,8,512]{3,2,1,0:T(8,128)} copy(f32[4,4,8,512]{3,2,1,0:T(8,128)S(1)} %cycle.1) | data formatting | bytes 524288

commit v3 on v2

--- a/solution.py
+++ b/solution.py
@@ -16,6 +16,7 @@
 ROWS, FIELDS, CHANNELS = 8, 4, 32
 PAIR = 2 * FIELDS
 TAPS = 48
+BIAS = 36
 HALVES = ((-3, 3), (-1, 3))
 
 
@@ -24,11 +25,13 @@
 
 
 def selections():
-    wide = np.zeros((4, 2 * TAPS, 9 * 3 * PAIR), np.float32)
-    narrow = np.zeros((2, 2 * TAPS, 6 * 3 * PAIR), np.float32)
+    wide = np.zeros((4, 2 * TAPS, 28 * PAIR), np.float32)
+    narrow = np.zeros((2, 2 * TAPS, 20 * PAIR), np.float32)
     for table, pairs in ((wide, 3), (narrow, 2)):
         third = pairs * 3 * PAIR
         for i in range(table.shape[0]):
+            table[i, BIAS, 3 * third] = 1.0
+            table[i, TAPS + BIAS, 3 * third + 1] = 1.0
             for k in range(pairs):
                 for b in range(3):
                     for f in range(FIELDS):
@@ -65,10 +68,6 @@
     return jnp.dot(a, b, preferred_element_type=F32)
 
 
-def three(ah, al, bh, bl):
-    return dot(ah, bh) + dot(al, bh) + dot(ah, bl)
-
-
 def cycle_kernel(
     inc_hbm, traj_hbm, *refs,
 ):
@@ -81,8 +80,8 @@
 def cycle(
     inc_hbm, traj_hbm, tables_hbm, corr, out, tables,
     inc, traj, up, down, top, bot,
-    taps_in, taps_out, bias, t1, t1n, t2h, t2l,
-    xs, hh, hl, fore, before, rows, cols, results, back, cmat,
+    taps_in, taps_out, t1, t1n, t2_first, t2_second,
+    ones, xs, hh, hl, fore, before, rows, cols, results, back, cmat,
     in_sem, table_sem, c_sem, met, halo_send, halo_recv, nb_send, nb_recv, f_send, f_recv, b_send, b_recv,
 ):
     slots, nx = inc.shape[0], inc.shape[3]
@@ -104,8 +103,9 @@
     def device(peer):
         return {"tm": peer[0] * width + peer[1]}
 
-    beside = [(my_field, strips[1]), (my_field, strips[-1])]
-    across = [(fields[1], my_row), (fields[-1], my_row)]
+    beside = [(my_field, strips[q]) for q in (2, -2)]
+    close = [(my_field, strips[q]) for q in (1, -1)]
+    across = [(fields[p], my_row) for p in range(1, FIELDS)]
 
     def say(sem, devices):
         for d in devices:
@@ -127,7 +127,7 @@
             pltpu.make_async_copy(inc_hbm.at[j], inc.at[j], in_sem.at[1, j]),
         )
 
-    say(barrier, beside + across)
+    say(barrier, beside + across + close)
     for j in order:
         for copy in inputs(j):
             copy.start()
@@ -163,7 +163,8 @@
             copy.wait()
         pack(j)
         if n == 0:
-            pl.semaphore_wait(barrier, 4 + jnp.minimum(place, 1) + jnp.minimum(last - place, 1))
+            pl.semaphore_wait(barrier, len(beside + across + close) + jnp.minimum(place, 1) + jnp.minimum(last - place, 1))
+            say(met.at[0], beside)
 
         @pl.when(place < last)
         def _():
@@ -173,8 +174,6 @@
         def _():
             to_previous(j).start()
 
-    rounds = width // 2 - 1
-    say(met.at[0], beside)
     for copy in table_copies:
         copy.wait()
 
@@ -187,32 +186,27 @@
             w = 0.5 * w_out[a, b]
             for q in range(4):
                 taps_out[q * TAPS + at : q * TAPS + at + FIELDS, q * CHANNELS : q * CHANNELS + CHANNELS] = w
-    taps_in[2 * TAPS : 2 * TAPS + 1, :CHANNELS] = w_bias[...]
+    taps_in[BIAS : BIAS + 1, :CHANNELS] = w_bias[...]
     w = taps_in[:TAPS, :]
     high = w.astype(BF16).astype(F32)
     taps_in[:TAPS, :] = high
     taps_in[TAPS : 2 * TAPS, :] = w - high
-    pl.semaphore_wait(met.at[0], 2)
-    say(met.at[1], beside)
     w = jnp.transpose(taps_in[...])[:CHANNELS]
-    bias[...] = jnp.broadcast_to(w[:, 2 * TAPS : 2 * TAPS + 1], (CHANNELS, 128))
     w = w[:, : 2 * TAPS].astype(BF16)
     for i in range(4):
         t1[CHANNELS * i : CHANNELS * i + CHANNELS, :] = dot(w, pick_wide[i]).astype(BF16)
     for i in range(2):
         t1n[CHANNELS * i : CHANNELS * i + CHANNELS, :] = dot(w, pick_narrow[i]).astype(BF16)
-    for n in range(1, rounds):
-        pl.semaphore_wait(met.at[n], 2)
-        say(met.at[n + 1], beside if n + 1 < rounds else across)
     lane_row = lax.shift_right_logical(lax.broadcasted_iota(jnp.int32, (1, 128), 1), 5) + place * ROWS
-    for part, target in zip(split(taps_out[...]), (t2h, t2l)):
+    for n, part in enumerate(split(taps_out[...])):
         for g in range(2):
             x = dot(pick_out[g], part)
-            for step_id in range(2):
+            for step_id, target in enumerate((t2_first, t2_second)):
+                lines = target.shape[1] // 2
                 for half in range(2):
                     row = lane_row + (HALVES[step_id][half] + 4 * g)
-                    keep = jnp.where((row >= 0) & (row < (last + 1) * ROWS), x, 0.0)
-                    target[step_id, half, :, 128 * g : 128 * g + 128] = keep.astype(BF16)
+                    keep = jnp.where((row >= 0) & (row < (last + 1) * ROWS), x[:lines], 0.0)
+                    target[half, n * lines : n * lines + lines, 128 * g : 128 * g + 128] = keep.astype(BF16)
 
     @pl.when(place == 0)
     def _():
@@ -222,8 +216,26 @@
     def _():
         bot[...] = jnp.zeros_like(bot)
 
-    column = lax.broadcasted_iota(jnp.int32, (1, nx), 1)
-    first, final = column == 0, column == nx - 1
+    pl.semaphore_wait(met.at[0], len(beside))
+    say(met.at[1], across)
+
+    column = lax.broadcasted_iota(jnp.int32, (1, 128), 1)
+    first, final = column == 0, column == 127
+
+    def from_left(x):
+        y = pltpu.roll(x, 1, 1)
+        return jnp.concatenate([jnp.where(first, 0.0, y[:, :128]), y[:, 128:]], axis=1)
+
+    def from_right(x):
+        y = pltpu.roll(x, nx - 1, 1)
+        return jnp.concatenate([y[:, : nx - 128], jnp.where(final, 0.0, y[:, nx - 128 :])], axis=1)
+
+    ones[...] = jnp.where(
+        (lax.broadcasted_iota(jnp.int32, ones.shape, 0) < 2)
+        & (lax.broadcasted_iota(jnp.int32, ones.shape, 1) < nx),
+        1.0,
+        0.0,
+    )
 
     def step(state, step_id):
         pairs = len(state[0])
@@ -234,30 +246,27 @@
             high, low = [], []
             for array in range(2):
                 x = state[array][k]
-                left = jnp.where(first, 0.0, pltpu.roll(x, 1, 1))
-                right = jnp.where(final, 0.0, pltpu.roll(x, nx - 1, 1))
-                x = jnp.concatenate([left, x, right], axis=0)
+                x = jnp.concatenate([from_left(x), x, from_right(x)], axis=0)
                 h = x.astype(BF16).astype(F32)
                 high.append(h)
                 low.append(x - h)
             highs.append(jnp.concatenate(high, axis=1))
             lows.append(jnp.concatenate(low, axis=1))
-        at = 0
         spans = [(g, 3) for g in range(0, pairs - 2, 2)] + [(pairs - 2, 2)]
         for g, n in spans:
             high = highs[g : g + n]
-            value = jnp.concatenate(high + lows[g : g + n] + high, axis=0).astype(BF16)
+            pad = [ones[:PAIR]] if n == 3 else [ones[...]]
+            value = jnp.concatenate(high + lows[g : g + n] + high + pad, axis=0).astype(BF16)
             xs[g // 2, : value.shape[0], :] = value
-        b = jnp.concatenate([bias[...], bias[...]], axis=1)[None]
         for n in range(0, nx, 256):
             s, t = slice(n, n + 256), slice(nx + n, nx + n + 256)
             at = 0
             for g, count in spans:
                 table, many = (t1, 4) if count == 3 else (t1n, 2)
-                depth_in = 9 * count * PAIR
+                depth_in = table.shape[1]
                 zs = dot(table[...], xs[g // 2, :depth_in, s])
                 zt = dot(table[...], xs[g // 2, :depth_in, t])
-                h = jnp.tanh(zs.reshape(many, CHANNELS, 256) + b).reshape(many * CHANNELS, 256)
+                h = jnp.tanh(zs)
                 slope = (1.0 - h * h) * zt
                 lines = slice(at, at + many * CHANNELS)
                 hh[lines, s], hl[lines, s] = split(h)
@@ -265,22 +274,17 @@
                 at += many * CHANNELS
         new = [[], []]
         wide, deep = outs // 2, (outs + 2) * CHANNELS
+        table = (t2_first, t2_second)[step_id]
         for array in range(2):
             lane = slice(array * nx, array * nx + nx)
             for half in range(2):
                 start = half * outs * CHANNELS
-                taps = three(
-                    t2h[step_id, half, : 3 * PAIR * wide, :deep],
-                    t2l[step_id, half, : 3 * PAIR * wide, :deep],
-                    hh[start : start + deep, lane],
-                    hl[start : start + deep, lane],
-                )
+                lines = 3 * PAIR * wide
+                both = dot(table[half, :, :deep], hh[start : start + deep, lane])
+                taps = both[:lines] + both[lines:] + dot(table[half, :lines, :deep], hl[start : start + deep, lane])
                 for k in range(wide):
-                    left = jnp.where(first, 0.0, pltpu.roll(taps[3 * PAIR * k : 3 * PAIR * k + PAIR], 1, 1))
-                    middle = taps[3 * PAIR * k + PAIR : 3 * PAIR * k + 2 * PAIR]
-                    right = pltpu.roll(taps[3 * PAIR * k + 2 * PAIR : 3 * PAIR * k + 3 * PAIR], nx - 1, 1)
-                    right = jnp.where(final, 0.0, right)
-                    new[array].append(state[array][half * wide + k + 1] + (left + middle + right))
+                    left, middle, right = (taps[PAIR * n : PAIR * n + PAIR] for n in range(3 * k, 3 * k + 3))
+                    new[array].append(state[array][half * wide + k + 1] + (from_left(left) + middle + from_right(right)))
         return new
 
     def line_of(peer):
@@ -288,8 +292,9 @@
         return lax.div(r, 2) * PAIR + 2 * f + lax.rem(r, 2)
 
     def send_residual(j, value):
+        lines = rows.reshape(slots * depth * quarter, 128)
         for q in range(quarter):
-            rows[j, :, q, :] = value[:, 128 * q : 128 * q + 128]
+            lines[pl.ds(j * depth * quarter + q, depth, stride=quarter), :] = value[:, 128 * q : 128 * q + 128]
         for peer in peers:
             pltpu.make_async_remote_copy(
                 rows.at[j, line_of(peer)], cols.at[j, me], f_send.at[j], f_recv.at[j],
@@ -323,19 +328,15 @@
         for array in range(2):
             state[array][0] = jnp.where(place > 0, state[array][0], 0.0)
             state[array][-1] = jnp.where(place < last, state[array][-1], 0.0)
+
         state = step(state, 1)
         forecast = jnp.concatenate(state[1], axis=0)
 
         @pl.when(i == 0)
         def _():
             fore[...] = forecast
-            pl.semaphore_wait(met.at[rounds], 2)
-            say(met.at[rounds + 1], across)
+            pl.semaphore_wait(met.at[1], len(across))
             to_after.start()
-
-        @pl.when(i == 1)
-        def _():
-            pl.semaphore_wait(met.at[rounds + 1], 2)
 
         @pl.when(i > 0)
         def _():
@@ -346,6 +347,7 @@
             to_after.wait()
             earlier = jnp.where(me == 0, 0.0, before[...])
             send_residual(0, increment_lines(0) - earlier)
+
 
     c_copy.wait()
     ch, cl = split(cmat[...])
@@ -353,9 +355,13 @@
     cl = dot(cl, perm[...]).astype(BF16)
     for j in range(slots):
         pltpu.make_async_copy(cols.at[j], cols.at[j], f_recv.at[j]).wait()
+    received = cols.reshape(slots * depth * quarter, 128)
+    sums = results.reshape(slots * depth * quarter, 128)
+    vh, vl = split(jnp.concatenate([received[pl.ds(q, slots * depth, stride=quarter), :] for q in range(quarter)], axis=1))
+    both = dot(jnp.concatenate([ch, cl], axis=0), vh)
+    total = both[: slots * depth] + both[slots * depth :] + dot(ch, vl)
     for q in range(quarter):
-        v = jnp.concatenate([cols[j, :, q, :] for j in range(slots)], axis=0)
-        results[:, q, :] = three(ch, cl, *split(v))
+        sums[pl.ds(q, slots * depth, stride=quarter), :] = total[:, 128 * q : 128 * q + 128]
     mine = pl.ds(me * slots, slots)
     for peer in peers:
         pltpu.make_async_remote_copy(
@@ -419,12 +425,12 @@
             pltpu.VMEM(halo, F32),
             pltpu.VMEM((128, 128), F32),
             pltpu.VMEM((4 * TAPS, 128), F32),
-            pltpu.VMEM((CHANNELS, 128), F32),
-            pltpu.VMEM((4 * CHANNELS, 27 * PAIR), BF16),
-            pltpu.VMEM((2 * CHANNELS, 18 * PAIR), BF16),
-            pltpu.VMEM((2, 2, 9 * PAIR, 256), BF16),
-            pltpu.VMEM((2, 2, 9 * PAIR, 256), BF16),
-            pltpu.VMEM((4, 27 * PAIR, 2 * nx), BF16),
+            pltpu.VMEM((4 * CHANNELS, 28 * PAIR), BF16),
+            pltpu.VMEM((2 * CHANNELS, 20 * PAIR), BF16),
+            pltpu.VMEM((2, 18 * PAIR, 256), BF16),
+            pltpu.VMEM((2, 12 * PAIR, 256), BF16),
+            pltpu.VMEM((2 * PAIR, 2 * nx), F32),
+            pltpu.VMEM((4, 28 * PAIR, 2 * nx), BF16),
             pltpu.VMEM(hidden, BF16),
             pltpu.VMEM(hidden, BF16),
             pltpu.VMEM((fields * rows, nx), F32),
@@ -434,7 +440,7 @@
             pltpu.VMEM((time, nx // 128, 128), F32),
             pltpu.VMEM((time, nx // 128, 128), F32),
             pltpu.VMEM((time, time), F32),
-            dma((2, slots)), dma((len(tables),)), dma, pltpu.SemaphoreType.REGULAR((8,)), dma((2, slots)), dma((2, slots)),
+            dma((2, slots)), dma((len(tables),)), dma, pltpu.SemaphoreType.REGULAR((2,)), dma((2, slots)), dma((2, slots)),
             dma, dma, dma((slots,)), dma((slots,)), dma, dma,
         ],
         compiler_params=pltpu.CompilerParams(collective_id=0, has_side_effects=True),

time: 35.2 us -> 34.5 us (0.980)
  the two profiles are of different devices: /device:TPU:8 before, /device:TPU:1 now
where the time goes in v3:
time: 34.5 us; the launch traced here: 34.4 us
  Pallas kernels  33.7 us (98%)
  local copies, waits for them, and re-layouts  0.71 us (2%)
    pallas_call x1, Pallas kernels, body(): pl.pallas_call(cycle_kernel, out_shape=pltpu.VMEM(local, F32), in_specs=[...  33.7 us
    unnamed x1, local copies, waits for them, and re-layouts  0.71 us

profile of v3, /device:TPU:1, one launch (start us, length us, event | category | flops | bytes accessed | tf_op | source)
XLA Modules:
  0.0 34.4 jit_solution(2163891211289833806)
XLA Ops:
  0.0 33.7 %cycle.1 = f32[4,4,8,512]{3,2,1,0:T(8,128)S(1)} custom-call(f32[4,4,8,512]{3,2,1,0:T(8,128)} %inc_hbm.1, f32[4,4,8,512]{3,2,1,0:T(8,128)} %traj_hbm.1, f32[3,3,4,32]{3,2,1,0:T(4,128)} %bitcast.3, f32[1,32]{1,0:T(1,128)} %bitcast.5, f32[3,3,4,32]{3,2,1,0:T(4,128)} %bitcast.4, bf16[4,96,224]{2,1,0:T(8,128)(2,1)} %constant.8.clone.refs_3_, ...), custom_call_target="tpu_custom_call" | custom-call | tf_op jit(solution)/shard_map/cycle/pallas_call | solution.py:413
  33.7 0.7 %copy.12 = f32[4,4,8,512]{3,2,1,0:T(8,128)} copy(f32[4,4,8,512]{3,2,1,0:T(8,128)S(1)} %cycle.1) | data formatting | bytes 524288

commit v4 on v3

--- a/solution.py
+++ b/solution.py
@@ -81,8 +81,8 @@
     inc_hbm, traj_hbm, tables_hbm, corr, out, tables,
     inc, traj, up, down, top, bot,
     taps_in, taps_out, t1, t1n, t2_first, t2_second,
-    ones, xs, hh, hl, fore, before, rows, cols, results, back, cmat,
-    in_sem, table_sem, c_sem, met, halo_send, halo_recv, nb_send, nb_recv, f_send, f_recv, b_send, b_recv,
+    ones, xs, hh, hl, rows_two, cols_two, rows, cols, results, back, cmat,
+    in_sem, table_sem, c_sem, met, halo_send, halo_recv, f_send, f_recv, b_send, b_recv,
 ):
     slots, nx = inc.shape[0], inc.shape[3]
     quarter = nx // 128
@@ -92,7 +92,7 @@
     my_field, my_row = lax.div(me, width), lax.rem(me, width)
     place = lax.axis_index("space")
     last = lax.axis_size("space") - 1
-    order = [slots - 1] + list(range(slots - 1))
+    order = range(slots)
 
     barrier = pltpu.get_barrier_semaphore()
 
@@ -291,26 +291,21 @@
         f, r = peer
         return lax.div(r, 2) * PAIR + 2 * f + lax.rem(r, 2)
 
-    def send_residual(j, value):
-        lines = rows.reshape(slots * depth * quarter, 128)
-        for q in range(quarter):
-            lines[pl.ds(j * depth * quarter + q, depth, stride=quarter), :] = value[:, 128 * q : 128 * q + 128]
+    def send_lines(phase, outgoing, incoming):
         for peer in peers:
             pltpu.make_async_remote_copy(
-                rows.at[j, line_of(peer)], cols.at[j, me], f_send.at[j], f_recv.at[j],
+                outgoing.at[line_of(peer)], incoming.at[me], f_send.at[phase], f_recv.at[phase],
                 device_id=device(peer), device_id_type=MESH,
             ).start()
-        pltpu.make_async_copy(rows.at[j, line_of((my_field, my_row))], cols.at[j, me], f_recv.at[j]).start()
+        own = outgoing.at[line_of((my_field, my_row))]
+        pltpu.make_async_copy(own, incoming.at[me], f_recv.at[phase]).start()
 
     def increment_lines(j):
         return jnp.concatenate([up[j, 1], down[j, 1]], axis=0)
 
-    after = lax.rem(me + 1, depth)
-    to_after = pltpu.make_async_remote_copy(fore, before, nb_send, nb_recv, device_id={"tm": after}, device_id_type=MESH)
-
     @pl.loop(0, slots)
     def _(i):
-        slot = lax.rem(i + slots - 1, slots)
+        slot = i
 
         @pl.when(place > 0)
         def _():
@@ -334,30 +329,42 @@
 
         @pl.when(i == 0)
         def _():
-            fore[...] = forecast
+            pair = (increment_lines(0), increment_lines(1) - forecast)
+            lines = rows_two.reshape(depth * 2 * quarter, 128)
+            for n, value in enumerate(pair):
+                for q in range(quarter):
+                    lines[pl.ds(n * quarter + q, depth, stride=2 * quarter), :] = value[:, 128 * q : 128 * q + 128]
             pl.semaphore_wait(met.at[1], len(across))
-            to_after.start()
+            send_lines(0, rows_two, cols_two)
 
         @pl.when(i > 0)
         def _():
-            send_residual(slot + 1, increment_lines(slot + 1) - forecast)
-
-        @pl.when(i == slots - 2)
-        def _():
-            to_after.wait()
-            earlier = jnp.where(me == 0, 0.0, before[...])
-            send_residual(0, increment_lines(0) - earlier)
-
+            following = increment_lines(jnp.minimum(i + 1, slots - 1))
+            value = jnp.where(i < slots - 1, following, 0.0) - forecast
+            lines = rows.reshape((slots - 1) * depth * quarter, 128)
+            for q in range(quarter):
+                lines[pl.ds((i - 1) * depth * quarter + q, depth, stride=quarter), :] = value[:, 128 * q : 128 * q + 128]
+            send_lines(i, rows.at[i - 1], cols.at[i - 1])
 
     c_copy.wait()
     ch, cl = split(cmat[...])
     ch = dot(ch, perm[...]).astype(BF16)
     cl = dot(cl, perm[...]).astype(BF16)
-    for j in range(slots):
-        pltpu.make_async_copy(cols.at[j], cols.at[j], f_recv.at[j]).wait()
-    received = cols.reshape(slots * depth * quarter, 128)
+    two = cols_two.reshape(depth * 2 * quarter, 128)
+    one = cols.reshape((slots - 1) * depth * quarter, 128)
     sums = results.reshape(slots * depth * quarter, 128)
-    vh, vl = split(jnp.concatenate([received[pl.ds(q, slots * depth, stride=quarter), :] for q in range(quarter)], axis=1))
+
+    def received(x, start, stride):
+        return jnp.concatenate([x[pl.ds(start + q, depth, stride=stride), :] for q in range(quarter)], axis=1)
+
+    pltpu.make_async_copy(cols_two, cols_two, f_recv.at[0]).wait()
+    values = [received(two, 0, 2 * quarter), received(two, quarter, 2 * quarter)]
+    for n in range(slots - 1):
+        pltpu.make_async_copy(cols.at[n], cols.at[n], f_recv.at[n + 1]).wait()
+        values.append(received(one, n * depth * quarter, quarter))
+    earlier = pltpu.roll(values.pop(), 1, 0)
+    values[0] += jnp.where(lax.broadcasted_iota(jnp.int32, earlier.shape, 0) == 0, 0.0, earlier)
+    vh, vl = split(jnp.concatenate(values, axis=0))
     both = dot(jnp.concatenate([ch, cl], axis=0), vh)
     total = both[: slots * depth] + both[slots * depth :] + dot(ch, vl)
     for q in range(quarter):
@@ -380,8 +387,11 @@
                 ]
     rest = pl.ds(0, (depth - 1) * slots)
     pltpu.make_async_copy(results.at[rest], results.at[rest], b_send).wait()
+    others = pl.ds(0, depth - 1)
+    pltpu.make_async_copy(rows_two.at[others], rows_two.at[others], f_send.at[0]).wait()
+    for n in range(slots - 1):
+        pltpu.make_async_copy(rows.at[n, others], rows.at[n, others], f_send.at[n + 1]).wait()
     for j in range(slots):
-        pltpu.make_async_copy(rows.at[j, pl.ds(0, depth - 1)], rows.at[j, pl.ds(0, depth - 1)], f_send.at[j]).wait()
 
         @pl.when(place < last)
         def _():
@@ -408,7 +418,7 @@
     local = increment.shape
     halo = (slots, 2, 2 * PAIR, nx)
     hidden = (14 * CHANNELS, 2 * nx)
-    message = (slots, depth, nx // 128, 128)
+    message = (slots - 1, depth, nx // 128, 128)
     dma = pltpu.SemaphoreType.DMA
     return pl.pallas_call(
         cycle_kernel,
@@ -433,15 +443,15 @@
             pltpu.VMEM((4, 28 * PAIR, 2 * nx), BF16),
             pltpu.VMEM(hidden, BF16),
             pltpu.VMEM(hidden, BF16),
-            pltpu.VMEM((fields * rows, nx), F32),
-            pltpu.VMEM((fields * rows, nx), F32),
+            pltpu.VMEM((depth, 2, nx // 128, 128), F32),
+            pltpu.VMEM((depth, 2, nx // 128, 128), F32),
             pltpu.VMEM(message, F32),
             pltpu.VMEM(message, F32),
             pltpu.VMEM((time, nx // 128, 128), F32),
             pltpu.VMEM((time, nx // 128, 128), F32),
             pltpu.VMEM((time, time), F32),
             dma((2, slots)), dma((len(tables),)), dma, pltpu.SemaphoreType.REGULAR((2,)), dma((2, slots)), dma((2, slots)),
-            dma, dma, dma((slots,)), dma((slots,)), dma, dma,
+            dma((slots,)), dma((slots,)), dma, dma,
         ],
         compiler_params=pltpu.CompilerParams(collective_id=0, has_side_effects=True),
         name="cycle",

time: 34.5 us -> 33.7 us (0.977)
  Pallas kernels: 33.7 us -> 32.9 us
    pallas_call x1, Pallas kernels: 33.7 us -> 32.9 us  [body(): pl.pallas_call(cycle_kernel, out_shape=pltpu.VMEM(local, F32), in_specs=[...]
where the time goes in v4:
time: 33.7 us; the launch traced here: 33.6 us
  Pallas kernels  32.9 us (98%)
  local copies, waits for them, and re-layouts  0.71 us (2%)
    pallas_call x1, Pallas kernels, body(): pl.pallas_call(cycle_kernel, out_shape=pltpu.VMEM(local, F32), in_specs=[...  32.9 us
    unnamed x1, local copies, waits for them, and re-layouts  0.71 us

profile of v4, /device:TPU:1, one launch (start us, length us, event | category | flops | bytes accessed | tf_op | source)
XLA Modules:
  0.0 33.6 jit_solution(8468521484428193226)
XLA Ops:
  0.0 32.9 %cycle.1 = f32[4,4,8,512]{3,2,1,0:T(8,128)S(1)} custom-call(f32[4,4,8,512]{3,2,1,0:T(8,128)} %inc_hbm.1, f32[4,4,8,512]{3,2,1,0:T(8,128)} %traj_hbm.1, f32[3,3,4,32]{3,2,1,0:T(4,128)} %bitcast.3, f32[1,32]{1,0:T(1,128)} %bitcast.5, f32[3,3,4,32]{3,2,1,0:T(4,128)} %bitcast.4, bf16[4,96,224]{2,1,0:T(8,128)(2,1)} %constant.8.clone.refs_3_, ...), custom_call_target="tpu_custom_call" | custom-call | tf_op jit(solution)/shard_map/cycle/pallas_call | solution.py:423
  32.9 0.7 %copy.12 = f32[4,4,8,512]{3,2,1,0:T(8,128)} copy(f32[4,4,8,512]{3,2,1,0:T(8,128)S(1)} %cycle.1) | data formatting | bytes 524288

commit v5 on v4

--- a/solution.py
+++ b/solution.py
@@ -81,7 +81,7 @@
     inc_hbm, traj_hbm, tables_hbm, corr, out, tables,
     inc, traj, up, down, top, bot,
     taps_in, taps_out, t1, t1n, t2_first, t2_second,
-    ones, xs, hh, hl, rows_two, cols_two, rows, cols, results, back, cmat,
+    ones, xs, hh, hl, rows_two, cols_two, rows, cols, results, partial, back, cmat,
     in_sem, table_sem, c_sem, met, halo_send, halo_recv, f_send, f_recv, b_send, b_recv,
 ):
     slots, nx = inc.shape[0], inc.shape[3]
@@ -348,27 +348,31 @@
 
     c_copy.wait()
     ch, cl = split(cmat[...])
-    ch = dot(ch, perm[...]).astype(BF16)
-    cl = dot(cl, perm[...]).astype(BF16)
+    both = jnp.concatenate([ch, cl], axis=0)
+    both = dot(both, perm[...]).astype(BF16)
+    time = slots * depth
     two = cols_two.reshape(depth * 2 * quarter, 128)
     one = cols.reshape((slots - 1) * depth * quarter, 128)
-    sums = results.reshape(slots * depth * quarter, 128)
+    sums = results.reshape(time * quarter, 128)
 
     def received(x, start, stride):
         return jnp.concatenate([x[pl.ds(start + q, depth, stride=stride), :] for q in range(quarter)], axis=1)
 
+    def product(columns, values):
+        vh, vl = split(values)
+        x = dot(both[:, columns], vh)
+        return x[:time] + x[time:] + dot(both[:time, columns], vl)
+
     pltpu.make_async_copy(cols_two, cols_two, f_recv.at[0]).wait()
     values = [received(two, 0, 2 * quarter), received(two, quarter, 2 * quarter)]
-    for n in range(slots - 1):
+    for n in range(slots - 2):
         pltpu.make_async_copy(cols.at[n], cols.at[n], f_recv.at[n + 1]).wait()
         values.append(received(one, n * depth * quarter, quarter))
-    earlier = pltpu.roll(values.pop(), 1, 0)
-    values[0] += jnp.where(lax.broadcasted_iota(jnp.int32, earlier.shape, 0) == 0, 0.0, earlier)
-    vh, vl = split(jnp.concatenate(values, axis=0))
-    both = dot(jnp.concatenate([ch, cl], axis=0), vh)
-    total = both[: slots * depth] + both[slots * depth :] + dot(ch, vl)
+    partial[...] = product(slice(0, time), jnp.concatenate(values, axis=0))
+    pltpu.make_async_copy(cols.at[slots - 2], cols.at[slots - 2], f_recv.at[slots - 1]).wait()
+    total = partial[...] + product(slice(time, time + depth), received(one, (slots - 2) * depth * quarter, quarter))
     for q in range(quarter):
-        sums[pl.ds(q, slots * depth, stride=quarter), :] = total[:, 128 * q : 128 * q + 128]
+        sums[pl.ds(q, time, stride=quarter), :] = total[:, 128 * q : 128 * q + 128]
     mine = pl.ds(me * slots, slots)
     for peer in peers:
         pltpu.make_async_remote_copy(
@@ -407,10 +411,12 @@
     pick_wide, pick_narrow, pick_out = (jnp.asarray(x, BF16) for x in selections())
     depth = lax.axis_size("tm")
     time = correlation.shape[1]
-    perm = np.zeros((time, time), np.float32)
+    perm = np.zeros((time, time + depth), np.float32)
     for e in range(depth):
         for j in range(slots):
             perm[e * slots + j, j * depth + e] = 1.0
+        if e + 1 < depth:
+            perm[(e + 1) * slots, time + e] = 1.0
     tables = (
         jnp.transpose(input_weight, (2, 3, 1, 0)), bias[None, :], jnp.transpose(output_weight, (2, 3, 0, 1)),
         pick_wide, pick_narrow, pick_out, jnp.asarray(perm, BF16),
@@ -448,6 +454,7 @@
             pltpu.VMEM(message, F32),
             pltpu.VMEM(message, F32),
             pltpu.VMEM((time, nx // 128, 128), F32),
+            pltpu.VMEM((time, nx), F32),
             pltpu.VMEM((time, nx // 128, 128), F32),
             pltpu.VMEM((time, time), F32),
             dma((2, slots)), dma((len(tables),)), dma, pltpu.SemaphoreType.REGULAR((2,)), dma((2, slots)), dma((2, slots)),

time: 33.7 us -> 33.7 us (level)
  no operation moved by 1% of the time
where the time goes in v5:
time: 33.7 us; the launch traced here: 33.6 us
  Pallas kernels  32.9 us (98%)
  local copies, waits for them, and re-layouts  0.71 us (2%)
    pallas_call x1, Pallas kernels, body(): pl.pallas_call(cycle_kernel, out_shape=pltpu.VMEM(local, F32), in_specs=[...  32.9 us
    unnamed x1, local copies, waits for them, and re-layouts  0.71 us

profile of v5, /device:TPU:1, one launch (start us, length us, event | category | flops | bytes accessed | tf_op | source)
XLA Modules:
  0.0 33.6 jit_solution(13939215530241355326)
XLA Ops:
  0.0 32.9 %cycle.1 = f32[4,4,8,512]{3,2,1,0:T(8,128)S(1)} custom-call(f32[4,4,8,512]{3,2,1,0:T(8,128)} %inc_hbm.1, f32[4,4,8,512]{3,2,1,0:T(8,128)} %traj_hbm.1, f32[3,3,4,32]{3,2,1,0:T(4,128)} %bitcast.3, f32[1,32]{1,0:T(1,128)} %bitcast.5, f32[3,3,4,32]{3,2,1,0:T(4,128)} %bitcast.4, bf16[4,96,224]{2,1,0:T(8,128)(2,1)} %constant.8.clone.refs_3_, ...), custom_call_target="tpu_custom_call" | custom-call | tf_op jit(solution)/shard_map/cycle/pallas_call | solution.py:429
  32.9 0.7 %copy.12 = f32[4,4,8,512]{3,2,1,0:T(8,128)} copy(f32[4,4,8,512]{3,2,1,0:T(8,128)S(1)} %cycle.1) | data formatting | bytes 524288

commit v6 on v5

--- a/solution.py
+++ b/solution.py
@@ -376,15 +376,16 @@
     mine = pl.ds(me * slots, slots)
     for peer in peers:
         pltpu.make_async_remote_copy(
-            results.at[pl.ds((peer[0] * width + peer[1]) * slots, slots)], back.at[mine], b_send, b_recv,
+            results.at[pl.ds((peer[0] * width + peer[1]) * slots, slots)], back.at[mine], b_send, b_recv.at[my_field],
             device_id=device(peer), device_id_type=MESH,
         ).start()
-    pltpu.make_async_copy(results.at[mine], back.at[mine], b_recv).start()
-
-    pltpu.make_async_copy(back, back, b_recv).wait()
+    pltpu.make_async_copy(results.at[mine], back.at[mine], b_recv.at[my_field]).start()
+
     lines = back.reshape(depth * slots * quarter, 128)
-    for j in range(slots):
-        for f in range(FIELDS):
+    for f in range(FIELDS):
+        group = back.at[pl.ds(f * width * slots, width * slots)]
+        pltpu.make_async_copy(group, group, b_recv.at[f]).wait()
+        for j in range(slots):
             for q in range(quarter):
                 out[j, f, :, 128 * q : 128 * q + 128] = lines[
                     pl.ds((f * width * slots + j) * quarter + q, ROWS, stride=slots * quarter), :
@@ -458,7 +459,7 @@
             pltpu.VMEM((time, nx // 128, 128), F32),
             pltpu.VMEM((time, time), F32),
             dma((2, slots)), dma((len(tables),)), dma, pltpu.SemaphoreType.REGULAR((2,)), dma((2, slots)), dma((2, slots)),
-            dma((slots,)), dma((slots,)), dma, dma,
+            dma((slots,)), dma((slots,)), dma, dma((FIELDS,)),
         ],
         compiler_params=pltpu.CompilerParams(collective_id=0, has_side_effects=True),
         name="cycle",

time: 33.7 us -> 33.8 us (level)
  no operation moved by 1% of the time
where the time goes in v6:
time: 33.8 us; the launch traced here: 33.7 us
  Pallas kernels  33 us (98%)
  local copies, waits for them, and re-layouts  0.71 us (2%)
    pallas_call x1, Pallas kernels, body(): pl.pallas_call(cycle_kernel, out_shape=pltpu.VMEM(local, F32), in_specs=[...  33 us
    unnamed x1, local copies, waits for them, and re-layouts  0.71 us

profile of v6, /device:TPU:1, one launch (start us, length us, event | category | flops | bytes accessed | tf_op | source)
XLA Modules:
  0.0 33.7 jit_solution(11953375158156239632)
XLA Ops:
  0.0 33.0 %cycle.1 = f32[4,4,8,512]{3,2,1,0:T(8,128)S(1)} custom-call(f32[4,4,8,512]{3,2,1,0:T(8,128)} %inc_hbm.1, f32[4,4,8,512]{3,2,1,0:T(8,128)} %traj_hbm.1, f32[3,3,4,32]{3,2,1,0:T(4,128)} %bitcast.3, f32[1,32]{1,0:T(1,128)} %bitcast.5, f32[3,3,4,32]{3,2,1,0:T(4,128)} %bitcast.4, bf16[4,96,224]{2,1,0:T(8,128)(2,1)} %constant.8.clone.refs_3_, ...), custom_call_target="tpu_custom_call" | custom-call | tf_op jit(solution)/shard_map/cycle/pallas_call | solution.py:430
  33.0 0.7 %copy.12 = f32[4,4,8,512]{3,2,1,0:T(8,128)} copy(f32[4,4,8,512]{3,2,1,0:T(8,128)S(1)} %cycle.1) | data formatting | bytes 524288

commit v7 on v5

--- a/solution.py
+++ b/solution.py
@@ -261,17 +261,18 @@
         for n in range(0, nx, 256):
             s, t = slice(n, n + 256), slice(nx + n, nx + n + 256)
             at = 0
+            made = []
             for g, count in spans:
                 table, many = (t1, 4) if count == 3 else (t1n, 2)
                 depth_in = table.shape[1]
-                zs = dot(table[...], xs[g // 2, :depth_in, s])
-                zt = dot(table[...], xs[g // 2, :depth_in, t])
+                made.append([dot(table[...], xs[g // 2, :depth_in, x]) for x in (s, t)])
+            for zs, zt in made:
                 h = jnp.tanh(zs)
                 slope = (1.0 - h * h) * zt
-                lines = slice(at, at + many * CHANNELS)
+                lines = slice(at, at + zs.shape[0])
                 hh[lines, s], hl[lines, s] = split(h)
                 hh[lines, t], hl[lines, t] = split(slope)
-                at += many * CHANNELS
+                at += zs.shape[0]
         new = [[], []]
         wide, deep = outs // 2, (outs + 2) * CHANNELS
         table = (t2_first, t2_second)[step_id]

time: 33.7 us -> 33.7 us (level)
  no operation moved by 1% of the time
where the time goes in v7:
time: 33.7 us; the launch traced here: 33.6 us
  Pallas kernels  32.9 us (98%)
  local copies, waits for them, and re-layouts  0.71 us (2%)
    pallas_call x1, Pallas kernels, body(): pl.pallas_call(cycle_kernel, out_shape=pltpu.VMEM(local, F32), in_specs=[...  32.9 us
    unnamed x1, local copies, waits for them, and re-layouts  0.71 us

profile of v7, /device:TPU:1, one launch (start us, length us, event | category | flops | bytes accessed | tf_op | source)
XLA Modules:
  0.0 33.6 jit_solution(4669951756382742723)
XLA Ops:
  0.0 32.9 %cycle.1 = f32[4,4,8,512]{3,2,1,0:T(8,128)S(1)} custom-call(f32[4,4,8,512]{3,2,1,0:T(8,128)} %inc_hbm.1, f32[4,4,8,512]{3,2,1,0:T(8,128)} %traj_hbm.1, f32[3,3,4,32]{3,2,1,0:T(4,128)} %bitcast.3, f32[1,32]{1,0:T(1,128)} %bitcast.5, f32[3,3,4,32]{3,2,1,0:T(4,128)} %bitcast.4, bf16[4,96,224]{2,1,0:T(8,128)(2,1)} %constant.8.clone.refs_3_, ...), custom_call_target="tpu_custom_call" | custom-call | tf_op jit(solution)/shard_map/cycle/pallas_call | solution.py:430
  32.9 0.7 %copy.12 = f32[4,4,8,512]{3,2,1,0:T(8,128)} copy(f32[4,4,8,512]{3,2,1,0:T(8,128)S(1)} %cycle.1) | data formatting | bytes 524288
